TPU v7x, 32 devices: a whole 2x2x4 slice. The times are simulated.
32 devices in a mesh: groups: 2 (over y), row: 8 (over z, x), col: 2 (over core).
Axes of the slice: x: 2, y: 2, z: 4, core: 2. Of those that a mesh axis runs over, the one named last changes fastest.
Arguments:
- tokens: bfloat16 [512, 8192], P(('groups', 'col'), 'row'), parts along dimension 0, may hold values from -6 to 6
- w_up: bfloat16 [8192, 32768], P('col', 'row'), may hold values from -0.125 to 0.125
- w_down: bfloat16 [32768, 8192], P('row', 'col'), may hold values from -0.0625 to 0.0625
- mask_up: int32 [64, 256], P(None, 'row'), may hold values 0 or 1
- mask_down: int32 [256, 64], P('row'), may hold values 0 or 1
Outputs:
- mixed: bfloat16 [512, 8192], P(('groups', 'col', 'row')), parts along dimension 0
There are 2 independent parts, one for each index of `groups`. A program takes and returns all parts, laid end to end along the dimension named above; an argument that names none is the same for every part. Nothing has to cross between parts.
All inputs are finite; a program needn't handle non-finite values. No bound on the sum of `mask_up` or of `mask_down` on one device may be relied on, other than what follows from the above.
Results may differ from a plain program's by a relative error of at most 0.005.
Values may be sent and summed in bfloat16 or wider, within the bound.
A program may use at most 512 MiB of HBM per device.

v0:
```python
import jax
import jax.numpy as jnp
from jax import lax
from jax.sharding import PartitionSpec as P


def expand_mask(mask, block, dtype):
    count_r, count_c = mask.shape
    wide = jnp.broadcast_to(mask.astype(dtype)[:, None, :, None], (count_r, block, count_c, block))
    return wide.reshape(count_r * block, count_c * block)


def per_device(tokens, w_up, w_down, mask_up, mask_down):
    width = w_up.shape[0] * lax.axis_size("col")
    block = width // mask_up.shape[0]
    up_full = lax.all_gather(w_up, "col", axis=0, tiled=True)
    up_masked = up_full * expand_mask(mask_up, block, up_full.dtype)
    pre = jnp.dot(
        lax.all_gather(tokens, "row", axis=1, tiled=True),
        up_masked,
        preferred_element_type=jnp.float32,
    )
    hidden = jax.nn.gelu(pre, approximate=False).astype(jnp.bfloat16)
    down_mask = expand_mask(mask_down, block, w_down.dtype)
    partial_sum = jnp.dot(
        hidden,
        lax.all_gather(w_down, "col", axis=1, tiled=True) * down_mask,
        preferred_element_type=jnp.float32,
    )
    mixed = lax.psum_scatter(partial_sum, "row", scatter_dimension=0, tiled=True).astype(
        jnp.bfloat16
    )
    return mixed


def solution(mesh):
    return jax.shard_map(
        per_device,
        mesh=mesh,
        in_specs=(
            P(("groups", "col"), "row"),
            P("col", "row"),
            P("row", "col"),
            P(None, "row"),
            P("row", None),
        ),
        out_specs=P(("groups", "col", "row"), None),
        check_vma=False,
    )
```

profile of v0, /device:TPU:0, one launch (start us, length us, event | category | flops | bytes accessed | tf_op | source)
XLA Modules:
  0.0 453.2 jit_solution(989160552235511673)
XLA Ops:
  6.5 0.0 all-gather.6.cloned.1.call-start
  6.5 0.7 all-gather.6.cloned.1.call-update
  7.3 0.0 all-gather.4.cloned.1.call-start
  7.3 0.7 all-gather.4.cloned.1.call-update
  8.0 0.0 copy-start
  8.0 0.0 copy-start.1
  8.0 0.0 all-gather.8.cloned.1.call-start
  8.1 0.7 all-gather.8.cloned.1.call-update
  8.8 0.0 reduce-scatter.2.cloned.1.call-start
  8.8 0.0 copy-done
  8.8 0.1 copy.6
  8.9 0.0 copy-done.1
  8.9 52.6 %all-gather.6.cloned.1.call-done = bf16[128,8192]{1,0:T(8,128)(2,1)} async-done(((bf16[128,1024]{1,0:T(8,128)(2,1)}), bf16[128,8192]{1,0:T(8,128)(2,1)}) %all-gather.6.cloned.1.call-update) | async-done | bytes 2097168 | tf_op jit(solution)/shard_map/all_gather | solution.py:19
  61.5 0.0 copy-start.2
  61.5 95.2 %all-gather.4.cloned.1.call-done = bf16[8192,4096]{1,0:T(8,128)(2,1)} async-done(((bf16[4096,4096]{1,0:T(8,128)(2,1)}), bf16[8192,4096]{1,0:T(8,128)(2,1)}) %all-gather.4.cloned.1.call-update) | async-done | bytes 67108880 | tf_op jit(solution)/shard_map/all_gather | solution.py:16
  156.7 37.8 %broadcast_in_dim.4 = bf16[64,128,32,128]{3,2,1,0:T(8,128)(2,1)} broadcast(bf16[64,32]{1,0:T(8,128)(2,1)S(1)} %copy.6), dimensions={0,2} | broadcast | bytes 67112960 | tf_op jit(solution)/shard_map/broadcast_in_dim | solution.py:9
  194.5 0.0 copy-done.2
  194.5 68.3 %fusion.2 = f32[4096,128]{1,0:T(8,128)} fusion(bf16[128,8192]{1,0:T(8,128)(2,1)S(1)} %copy-done.2, bf16[8192,4096]{1,0:T(8,128)(2,1)} %all-gather.4.cloned.1.call-done, bf16[1024,8,32,128]{3,2,1,0:T(8,128)(2,1)} %bitcast.3), kind=kOutput, calls=%fused_computation.4 | convolution fusion | flops 8623489024 | bytes 138412032 | tf_op jit(solution)/shard_map/dot_general | solution.py:18
  262.8 0.0 copy-start.3
  262.8 0.0 all-gather.8.cloned.1.call-done
  262.8 21.4 %broadcast_in_dim.5 = bf16[32,128,64,128]{3,2,1,0:T(8,128)(2,1)} broadcast(bf16[32,64]{1,0:T(8,128)(2,1)S(1)} %convert_element_type.14), dimensions={0,2} | broadcast | bytes 67112960 | tf_op jit(solution)/shard_map/broadcast_in_dim | solution.py:9
  284.3 0.0 copy-done.3
  284.3 71.4 %fusion = f32[128,8192]{1,0:T(8,128)} fusion(bf16[4096,8192]{1,0:T(8,128)(2,1)} %all-gather.8.cloned.1.call-done, bf16[512,8,64,128]{3,2,1,0:T(8,128)(2,1)} %bitcast.6, f32[4096,128]{1,0:T(8,128)S(1)} %copy-done.3), kind=kOutput, calls=%fused_computation.1 | convolution fusion | flops 8657567744 | bytes 140509184 | tf_op jit(solution)/shard_map/dot_general | solution.py:25
  355.7 0.0 reduce-scatter.2.cloned.1.call-update
  355.7 89.2 %reduce-scatter.2.cloned.1.call-done = f32[16,8192]{1,0:T(8,128)} async-done(((f32[128,8192]{1,0:T(8,128)}), f32[16,8192]{1,0:T(8,128)}) %reduce-scatter.2.cloned.1.call-update) | async-done | bytes 524304 | tf_op jit(solution)/shard_map/reduce_scatter | solution.py:30
  444.9 1.8 convert_element_type.15
  (2 shorter events, 0.0 us)
Async XLA Ops:
  6.5 55.0 %all-gather.6.cloned.1.call-start = ((), (), s32[]{:S(2)}) async-start(), calls=%async_computation.2 | async-start | bytes 2359296 | tf_op jit(solution)/shard_map/all_gather | solution.py:19
  7.3 149.5 %all-gather.4.cloned.1.call-start = ((), (), s32[]{:S(2)}) async-start(), calls=%async_computation.1 | async-start | bytes 100663296 | tf_op jit(solution)/shard_map/all_gather | solution.py:16
  8.0 0.8 copy-start
  8.0 0.9 copy-start.1
  8.0 254.8 %all-gather.8.cloned.1.call-start = ((), (), s32[]{:S(2)}) async-start(), calls=%async_computation.3 | async-start | bytes 100663296 | tf_op jit(solution)/shard_map/all_gather | solution.py:27
  8.8 436.1 %reduce-scatter.2.cloned.1.call-start = ((), (), s32[]{:S(2)}) async-start(), calls=%async_computation.4 | async-start | bytes 4718592 | tf_op jit(solution)/shard_map/reduce_scatter | solution.py:30
  61.5 133.0 %copy-start.2 = (bf16[128,8192]{1,0:T(8,128)(2,1)S(1)}, bf16[128,8192]{1,0:T(8,128)(2,1)}, u32[]{:S(2)}) copy-start(bf16[128,8192]{1,0:T(8,128)(2,1)} %all-gather.6.cloned.1.call-done) | copy-start | bytes 6291460
  262.8 21.4 %copy-start.3 = (f32[4096,128]{1,0:T(8,128)S(1)}, f32[4096,128]{1,0:T(8,128)}, u32[]{:S(2)}) copy-start(f32[4096,128]{1,0:T(8,128)} %fusion.2) | copy-start | bytes 6291460
Sparse Core Ops, SparseCore 0:
  9.5 51.9 all-gather.5
  63.1 93.5 all-gather.3
  158.3 96.2 all-gather.7
  355.8 89.0 reduce-scatter.1
where the time goes:
time: 453 us
  waiting for transfers between devices  239 us (53%)
  matrix products  140 us (31%)
  local copies, waits for them, and re-layouts  59.3 us (13%)
  between operations  13.2 us (3%)
    all_gather x1, waiting for transfers between devices, per_device(): up_full = lax.all_gather(w_up, 'col', axis=0, tiled=True)  95.2 us
    reduce_scatter x1, waiting for transfers between devices, per_device(): lax.psum_scatter(partial_sum, 'row', scatter_dimension=0, tiled=True)  89.2 us
    dot_general x1, matrix products, per_device(): jnp.dot(hidden, lax.all_gather(w_down, 'col', axis=1, tiled=True) * down_...  71.4 us
    dot_general x1, matrix products, per_device(): jnp.dot(lax.all_gather(tokens, 'row', axis=1, tiled=True), up_masked, pre...  68.3 us
    broadcast_in_dim x2, local copies, waits for them, and re-layouts, expand_mask(): jnp.broadcast_to(mask.astype(dtype)[:, None, :, None], (count_r, block, c...  59.2 us
    all_gather x1, waiting for transfers between devices, per_device(): lax.all_gather(tokens, 'row', axis=1, tiled=True)  52.6 us
  transfers between devices with their start and end apart: 4, of which 3 were waited for; matrix products, arithmetic and copies ran while one was open for 23% of the time, Pallas kernels for 0%

commit v1 on v0

v1 whole, which is shorter than its diff:
```python
import jax
import jax.numpy as jnp
from jax import lax
from jax.sharding import PartitionSpec as P


def expand_mask(mask, block, dtype):
    count_r, count_c = mask.shape
    wide = jnp.broadcast_to(mask.astype(dtype)[:, None, :, None], (count_r, block, count_c, block))
    return wide.reshape(count_r * block, count_c * block)


def per_device(tokens, w_up, w_down, mask_up, mask_down):
    cols = lax.axis_size("col")
    block = w_up.shape[0] * cols // mask_up.shape[0]
    core = lax.axis_index("col")
    mine = lax.all_gather(tokens, "row", axis=1, tiled=True)
    x = lax.all_to_all(mine, "col", split_axis=1, concat_axis=0, tiled=True)
    half = mask_up.shape[0] // cols
    mask_u = lax.dynamic_slice_in_dim(mask_up, core * half, half, 0)
    pre = jnp.dot(
        x, w_up * expand_mask(mask_u, block, w_up.dtype), preferred_element_type=jnp.float32
    )
    swap = [(i, (i + 1) % cols) for i in range(cols)]
    pre = pre + lax.ppermute(pre.astype(jnp.bfloat16), "col", swap).astype(jnp.float32)
    hidden = jax.nn.gelu(pre, approximate=False).astype(jnp.bfloat16)
    half_d = mask_down.shape[1] // cols
    mask_d = lax.dynamic_slice_in_dim(mask_down, core * half_d, half_d, 1)
    part = jnp.dot(
        hidden,
        w_down * expand_mask(mask_d, block, w_down.dtype),
        preferred_element_type=jnp.float32,
    )
    part = lax.all_to_all(
        part.astype(jnp.bfloat16), "col", split_axis=0, concat_axis=1, tiled=True
    )
    return lax.psum_scatter(part, "row", scatter_dimension=0, tiled=True).astype(jnp.bfloat16)


def solution(mesh):
    return jax.shard_map(
        per_device,
        mesh=mesh,
        in_specs=(
            P(("groups", "col"), "row"),
            P("col", "row"),
            P("row", "col"),
            P(None, "row"),
            P("row", None),
        ),
        out_specs=P(("groups", "col", "row"), None),
        check_vma=False,
    )
```

time: 453 us -> 249 us (0.55)
  waiting for transfers between devices: 239 us -> 123 us
  matrix products: 140 us -> 70.2 us
  local copies, waits for them, and re-layouts: 59.3 us -> 28.4 us
  blocking collectives: 0 us -> 12 us
    all_gather x3 -> x1, waiting for transfers between devices: 148 us -> 52.2 us  [per_device(): mine = lax.all_gather(tokens, 'row', axis=1, tiled=True)]
    dot_general x2, matrix products: 140 us -> 70.2 us  [the longest x1 36.5 us: per_device(): jnp.dot(hidden, w_down * expand_mask(mask_d, block, w_down.dtype), prefer...]
    broadcast_in_dim x2, local copies, waits for them, and re-layouts: 59.2 us -> 22.3 us  [expand_mask(): jnp.broadcast_to(mask.astype(dtype)[:, None, :, None], (count_r, block, c...]
    reduce_scatter x1, waiting for transfers between devices: 89.2 us -> 66.9 us  [per_device(): lax.psum_scatter(part, 'row', scatter_dimension=0, tiled=True)]
    all_to_all x0 -> x2, blocking collectives: none -> 12 us  [the longest x1 6.61 us: per_device(): x = lax.all_to_all(mine, 'col', split_axis=1, concat_axis=0, tiled=True)]
  transfers between devices with their start and end apart: 4 -> 3, of which waited for: 3 -> 3; matrix products, arithmetic and copies ran while one was open for 23% -> 0% of each run, Pallas kernels for 0% -> 0%
where the time goes in v1:
time: 249 us; the launch traced here: 248 us
  waiting for transfers between devices  123 us (49%)
  matrix products  70.2 us (28%)
  local copies, waits for them, and re-layouts  28.4 us (11%)
  between operations  13.4 us (5%)
  blocking collectives  12 us (5%)
    reduce_scatter x1, waiting for transfers between devices, per_device(): lax.psum_scatter(part, 'row', scatter_dimension=0, tiled=True)  66.9 us
    all_gather x1, waiting for transfers between devices, per_device(): mine = lax.all_gather(tokens, 'row', axis=1, tiled=True)  52.2 us
    dot_general x1, matrix products, per_device(): jnp.dot(hidden, w_down * expand_mask(mask_d, block, w_down.dtype), prefer...  36.5 us
    dot_general x1, matrix products, per_device(): jnp.dot(x, w_up * expand_mask(mask_u, block, w_up.dtype), preferred_eleme...  33.7 us
    broadcast_in_dim x2, local copies, waits for them, and re-layouts, expand_mask(): jnp.broadcast_to(mask.astype(dtype)[:, None, :, None], (count_r, block, c...  22.3 us
    all_to_all x1, blocking collectives, per_device(): x = lax.all_to_all(mine, 'col', split_axis=1, concat_axis=0, tiled=True)  6.61 us
    all_to_all x1, blocking collectives, per_device(): lax.all_to_all(part.astype(jnp.bfloat16), 'col', split_axis=0, concat_axi...  5.42 us
  transfers between devices with their start and end apart: 3, of which 3 were waited for; matrix products, arithmetic and copies ran while one was open for 0% of the time, Pallas kernels for 0%

profile of v1, /device:TPU:0, one launch (start us, length us, event | category | flops | bytes accessed | tf_op | source)
XLA Modules:
  0.0 248.3 jit_solution(15426954880233412906)
XLA Ops:
  6.5 0.0 all-gather.2.cloned.1.call-start
  6.5 1.8 copy.11
  8.3 0.0 all-gather.2.cloned.1.call-update
  8.4 0.0 reduce-scatter.2.cloned.1.call-start
  8.4 0.8 dynamic-slice_convert_fusion.1
  9.2 0.1 copy.10
  9.3 52.2 %all-gather.2.cloned.1.call-done = bf16[128,8192]{0,1:T(8,128)(2,1)} async-done(((bf16[128,1024]{0,1:T(8,128)(2,1)}), bf16[128,8192]{0,1:T(8,128)(2,1)}) %all-gather.2.cloned.1.call-update) | async-done | bytes 2097168 | tf_op jit(solution)/shard_map/all_gather | solution.py:17
  61.5 6.6 %all_to_all.38 = bf16[128,2,4096]{0,2,1:T(8,128)(2,1)S(1)} all-to-all(bf16[128,2,4096]{0,2,1:T(8,128)(2,1)} %bitcast.31), channel_id=1, replica_groups=mesh['groups'=2,'row'=8,'col'=2] {'col'}, dimensions={1} | all-to-all | bytes 4194304 | tf_op jit(solution)/shard_map/all_to_all | solution.py:18
  68.1 2.7 %copy.12 = bf16[2,128,4096]{2,1,0:T(8,128)(2,1)} copy(bf16[2,128,4096]{1,2,0:T(8,128)(2,1)S(1)} %bitcast.29) | data formatting | bytes 4194304 | tf_op jit(solution)/shard_map/all_to_all | solution.py:18
  70.9 0.0 copy-start
  70.9 11.1 %broadcast_in_dim.4 = bf16[32,128,32,128]{3,2,1,0:T(8,128)(2,1)} broadcast(bf16[32,32]{1,0:T(8,128)(2,1)S(1)} %copy.10), dimensions={0,2} | broadcast | bytes 33556480 | tf_op jit(solution)/shard_map/broadcast_in_dim | solution.py:9
  82.0 0.0 copy-done
  82.0 0.0 copy-start.1
  82.0 33.7 %fusion.77 = (bf16[256,4096]{0,1:T(8,128)(2,1)}, f32[256,4096]{0,1:T(8,128)}) fusion(bf16[256,4096]{1,0:T(8,128)(2,1)S(1)} %bitcast.32, bf16[4096,4096]{1,0:T(8,128)(2,1)} %param.6, bf16[512,8,32,128]{3,2,1,0:T(8,128)(2,1)} %bitcast.26), kind=kOutput, calls=%fused_computation.90 | convolution fusion | flops 8607760384 | bytes 75497472 | tf_op jit(solution)/shard_map/dot_general | solution.py:21
  115.7 0.1 collective-permute-start
  115.9 0.0 copy-done.1
  115.9 0.1 dynamic-slice_convert_fusion
  115.9 4.2 %collective-permute-done = bf16[256,4096]{0,1:T(8,128)(2,1)S(1)} collective-permute-done((bf16[256,4096]{0,1:T(8,128)(2,1)}, bf16[256,4096]{0,1:T(8,128)(2,1)S(1)}, u32[]{:S(2)}, u32[]{:S(2)}) %collective-permute-start) | collective-permute-done | bytes 2097184 | tf_op jit(solution)/shard_map/ppermute | solution.py:25
  120.1 11.1 %broadcast_in_dim.5 = bf16[32,128,32,128]{3,2,1,0:T(8,128)(2,1)} broadcast(bf16[32,32]{1,0:T(8,128)(2,1)S(1)} %dynamic-slice_convert_fusion), dimensions={0,2} | broadcast | bytes 33556480 | tf_op jit(solution)/shard_map/broadcast_in_dim | solution.py:9
  131.2 36.5 %fusion.5 = bf16[256,4096]{1,0:T(8,128)(2,1)S(1)} fusion(bf16[4096,4096]{1,0:T(8,128)(2,1)} %param.7, bf16[512,8,32,128]{3,2,1,0:T(8,128)(2,1)} %bitcast.27, f32[256,4096]{0,1:T(8,128)} %get-tuple-element.6, bf16[256,4096]{0,1:T(8,128)(2,1)S(1)} %collective-permute-done), kind=kOutput, calls=%fused_computation.8 | convolution fusion | flops 8678014976 | bytes 75497472 | tf_op jit(solution)/shard_map/dot_general | solution.py:29
  167.7 5.4 %all_to_all.39 = bf16[2,128,4096]{2,1,0:T(8,128)(2,1)S(1)} all-to-all(bf16[2,128,4096]{2,1,0:T(8,128)(2,1)S(1)} %bitcast.33), channel_id=1, replica_groups=mesh['groups'=2,'row'=8,'col'=2] {'col'}, dimensions={0} | all-to-all | bytes 4194304 | tf_op jit(solution)/shard_map/all_to_all | solution.py:34
  173.1 1.5 copy.14
  174.6 0.0 reduce-scatter.2.cloned.1.call-update
  174.6 66.9 %reduce-scatter.2.cloned.1.call-done = bf16[16,8192]{1,0:T(8,128)(2,1)} async-done(((bf16[128,8192]{1,0:T(8,128)(2,1)}), bf16[16,8192]{1,0:T(8,128)(2,1)}) %reduce-scatter.2.cloned.1.call-update) | async-done | bytes 262160 | tf_op jit(solution)/shard_map/reduce_scatter | solution.py:37
Async XLA Ops:
  6.5 55.0 %all-gather.2.cloned.1.call-start = ((), (), s32[]{:S(2)}) async-start(), calls=%async_computation.3 | async-start | bytes 2359296 | tf_op jit(solution)/shard_map/all_gather | solution.py:17
  8.4 233.2 %reduce-scatter.2.cloned.1.call-start = ((), (), s32[]{:S(2)}) async-start(), calls=%async_computation.4 | async-start | bytes 2359296 | tf_op jit(solution)/shard_map/reduce_scatter | solution.py:37
  70.9 11.1 %copy-start = (bf16[2,128,4096]{2,1,0:T(8,128)(2,1)S(1)}, bf16[2,128,4096]{2,1,0:T(8,128)(2,1)}, u32[]{:S(2)}) copy-start(bf16[2,128,4096]{2,1,0:T(8,128)(2,1)} %copy.12) | copy-start | bytes 6291460
  82.0 33.9 %copy-start.1 = (s32[32,64]{1,0:T(8,128)S(1)}, s32[32,64]{1,0:T(8,128)}, u32[]{:S(2)}) copy-start(s32[32,64]{1,0:T(8,128)} %param.9) | copy-start | bytes 24580
  115.7 4.4 %collective-permute-start = (bf16[256,4096]{0,1:T(8,128)(2,1)}, bf16[256,4096]{0,1:T(8,128)(2,1)S(1)}, u32[]{:S(2)}, u32[]{:S(2)}) collective-permute-start(bf16[256,4096]{0,1:T(8,128)(2,1)} %get-tuple-element.5), channel_id=1, source_target_pairs={{0,1},{1,0},{2,3},{3,2},{4,5},{5,4},{6,7},{7,6},{8,9},{9,8},{10,11... | collective-permute-start | bytes 6291464 | tf_op jit(solution)/shard_map/ppermute | solution.py:25
Sparse Core Ops, SparseCore 0:
  9.5 51.9 all-gather.1
  174.8 66.7 reduce-scatter.1

commit v2 on v1

--- a/solution.py
+++ b/solution.py
@@ -1,6 +1,10 @@
+import functools
+
 import jax
 import jax.numpy as jnp
 from jax import lax
+from jax.experimental import pallas as pl
+from jax.experimental.pallas import tpu as pltpu
 from jax.sharding import PartitionSpec as P
 
 
@@ -10,7 +14,7 @@
     return wide.reshape(count_r * block, count_c * block)
 
 
-def per_device(tokens, w_up, w_down, mask_up, mask_down):
+def general(tokens, w_up, w_down, mask_up, mask_down):
     cols = lax.axis_size("col")
     block = w_up.shape[0] * cols // mask_up.shape[0]
     core = lax.axis_index("col")
@@ -35,6 +39,348 @@
         part.astype(jnp.bfloat16), "col", split_axis=0, concat_axis=1, tiled=True
     )
     return lax.psum_scatter(part, "row", scatter_dimension=0, tiled=True).astype(jnp.bfloat16)
+
+
+MESH = pl.DeviceIdType.MESH
+BF16, F32 = jnp.bfloat16, jnp.float32
+LAG = 2
+
+
+def gelu(v):
+    return 0.5 * v * (1.0 + lax.erf(v * 0.7071067811865476))
+
+
+def kernel(
+    block,
+    tokens, w_up, w_down, mask_up, mask_down,
+    out,
+    w, x_all, acc, other, hid, part, own, to_x, from_x, to_z, from_left, from_right, final,
+    load_sem, w_sem, x_send, x_recv, pre_send, pre_recv, hid_send, hid_recv,
+    rs_send, rs_recv, right_send, right_recv, left_send, left_recv, out_sem,
+):
+    row, core = lax.axis_index("row"), lax.axis_index("col")
+    z, x = row // 2, row % 2
+    chunks, depth, wide = w.shape
+    feats = x_all.shape[-1]
+    half = chunks * wide
+    count = 8
+
+    def loop(steps, body):
+        lax.fori_loop(0, steps, lambda i, _: (body(i), 0)[1], 0)
+
+    def cols(n):
+        return pl.ds(pl.multiple_of(n * wide, wide), wide)
+
+    def load_w(source, n):
+        return pltpu.make_async_copy(source.at[:, cols(n)], w.at[n], w_sem.at[n])
+
+    loop(chunks, lambda n: load_w(w_up, n).start())
+    load = pltpu.make_async_copy(tokens, x_all.at[row, core], load_sem)
+    load.start()
+
+    barrier = pltpu.get_barrier_semaphore()
+    right, left = {"row": row + 2}, {"row": row - 2}
+    across, mate = {"row": z * 2 + 1 - x}, {"col": 1 - core}
+    has_right, has_left = z < 3, z > 0
+
+    def greet(device):
+        pl.semaphore_signal(barrier, inc=1, device_id=device, device_id_type=MESH)
+
+    greet(across)
+    greet(mate)
+    pl.when(has_right)(lambda: greet(right))
+    pl.when(has_left)(lambda: greet(left))
+    ends = jnp.where(has_right, 1, 0) + jnp.where(has_left, 1, 0)
+    pl.semaphore_wait(barrier, 2 + ends)
+    load.wait()
+
+    def copy_x(kind, r, device, which):
+        return pltpu.make_async_remote_copy(
+            src_ref=x_all.at[r, which], dst_ref=x_all.at[r, which],
+            send_sem=x_send.at[kind, r], recv_sem=x_recv.at[r, which],
+            device_id=device, device_id_type=MESH,
+        )
+
+    def to_mate(zp, xp):
+        @pl.when(zp // 2 == 1 - core)
+        def _():
+            copy_x(3, zp * 2 + xp, mate, core).start()
+
+    def pass_on(zp, go_right, go_left):
+        r = zp * 2 + x
+        pl.when(go_right)(lambda: copy_x(0, r, right, core).start())
+        pl.when(go_left)(lambda: copy_x(1, r, left, core).start())
+        copy_x(2, r, across, core).start()
+        to_mate(zp, x)
+
+    def arrive(zp, xp):
+        copy_x(2, zp * 2 + xp, across, core).wait_recv()
+
+    pass_on(z, has_right, has_left)
+
+    def step(d):
+        if d < 4:
+
+            @pl.when(z - d >= 0)
+            def _():
+                arrive(z - d, x)
+                pass_on(z - d, has_right, False)
+
+            @pl.when(z + d <= 3)
+            def _():
+                arrive(z + d, x)
+                pass_on(z + d, False, has_left)
+
+        @pl.when(z - (d - 1) >= 0)
+        def _():
+            arrive(z - (d - 1), 1 - x)
+            to_mate(z - (d - 1), 1 - x)
+
+        if d > 1:
+
+            @pl.when(z + (d - 1) <= 3)
+            def _():
+                arrive(z + (d - 1), 1 - x)
+                to_mate(z + (d - 1), 1 - x)
+
+    def copy_pre(n):
+        return pltpu.make_async_remote_copy(
+            src_ref=acc.at[n, 1 - core], dst_ref=other.at[n],
+            send_sem=pre_send.at[n], recv_sem=pre_recv.at[n],
+            device_id=mate, device_id_type=MESH,
+        )
+
+    def masked(n, start, mask, blocks):
+        parts = []
+        for j in range(blocks):
+            keep = mask[pl.ds(start + j, 1), cols(n)].astype(BF16)
+            rows = pl.ds(pl.multiple_of((start + j) * block, block), block)
+            parts.append(w[n, rows, :] * keep)
+        return jnp.concatenate(parts, axis=0)
+
+    def up(r, first, last):
+        copy_x(3, r, mate, 1 - core).wait_recv()
+        blocks = feats // block
+        start = (r - 4 * core) * blocks
+
+        def body(n):
+            if first:
+                load_w(w_up, n).wait()
+            done = jnp.dot(
+                x_all[r].reshape(-1, feats), masked(n, start, mask_up, blocks),
+                preferred_element_type=F32,
+            ).reshape(acc.shape[1:])
+            acc[n] = done if first else acc[n] + done
+            if last:
+                copy_pre(n).start()
+                load_w(w_down, n).start()
+
+        loop(chunks, body)
+
+    low = 2 * core
+    near = jnp.clip(z, low, low + 1)
+    far = 2 * low + 1 - near
+    step(1)
+    step(2)
+    up(near * 2 + x, True, False)
+    step(3)
+    up(far * 2 + x, False, False)
+    up(near * 2 + 1 - x, False, False)
+    step(4)
+    up(far * 2 + 1 - x, False, True)
+
+    def copy_hid(n, which):
+        return pltpu.make_async_remote_copy(
+            src_ref=hid.at[n, which], dst_ref=hid.at[n, which],
+            send_sem=hid_send.at[n], recv_sem=hid_recv.at[n],
+            device_id=mate, device_id_type=MESH,
+        )
+
+    def finish(n):
+        copy_pre(n).wait_recv()
+        hid[n, core] = gelu(acc[n, core] + other[n]).astype(BF16)
+        copy_hid(n, core).start()
+
+    loop(chunks, finish)
+    loop(chunks, lambda n: copy_hid(n, 1 - core).wait_recv())
+
+    def copy_rs(n):
+        return pltpu.make_async_remote_copy(
+            src_ref=to_x.at[n], dst_ref=from_x.at[n],
+            send_sem=rs_send.at[n], recv_sem=rs_recv.at[n],
+            device_id=across, device_id_type=MESH,
+        )
+
+    def copy_right(n, zp):
+        return pltpu.make_async_remote_copy(
+            src_ref=to_z.at[n, zp], dst_ref=from_left.at[n, zp],
+            send_sem=right_send.at[n, zp], recv_sem=right_recv.at[n, zp],
+            device_id=right, device_id_type=MESH,
+        )
+
+    def copy_left(n, zp):
+        return pltpu.make_async_remote_copy(
+            src_ref=to_z.at[n, zp], dst_ref=from_right.at[n, zp],
+            send_sem=left_send.at[n, zp], recv_sem=left_recv.at[n, zp],
+            device_id=left, device_id_type=MESH,
+        )
+
+    def down(n):
+        load_w(w_down, n).wait()
+        part[...] = jnp.zeros_like(part)
+        blocks = wide // block
+
+        def body(k):
+            part[...] += jnp.dot(
+                hid[k].reshape(-1, wide), masked(n, k * blocks, mask_down, blocks),
+                preferred_element_type=F32,
+            ).reshape(part.shape)
+
+        loop(depth // wide, body)
+        for zp in range(4):
+            for cp in range(2):
+                to_x[n, zp, cp] = part[cp, zp, 1 - x].astype(BF16)
+        copy_rs(n).start()
+        for zp in range(4):
+            for cp in range(2):
+                own[n, zp, cp] = part[cp, zp, x]
+
+    def take_x(n):
+        copy_rs(n).wait_recv()
+        own[n] = own[n] + from_x[n].astype(F32)
+
+    def go_right(n):
+        for zp in (3, 2, 1, 0):
+
+            @pl.when(has_left & (zp >= z))
+            def _():
+                copy_right(n, zp).wait_recv()
+                own[n, zp] = own[n, zp] + from_left[n, zp].astype(F32)
+
+            @pl.when(zp > z)
+            def _():
+                to_z[n, zp] = own[n, zp].astype(BF16)
+                copy_right(n, zp).start()
+
+    def go_left(n):
+        for zp in (0, 1, 2, 3):
+
+            @pl.when(has_right & (zp <= z))
+            def _():
+                copy_left(n, zp).wait_recv()
+                own[n, zp] = own[n, zp] + from_right[n, zp].astype(F32)
+
+            @pl.when(zp < z)
+            def _():
+                to_z[n, zp] = own[n, zp].astype(BF16)
+                copy_left(n, zp).start()
+
+    def pipeline(i):
+        for n, stage in (
+            (i, down), (i - LAG, take_x), (i - LAG - z, go_right), (i - LAG - 3 + z, go_left),
+        ):
+            pl.when((n >= 0) & (n < chunks))(functools.partial(stage, n))
+
+    loop(chunks + LAG + 3, pipeline)
+
+    def store(n):
+        final[:, cols(n)] = own[n, z, 1 - core].astype(BF16)
+        place = pl.ds(pl.multiple_of(core * half + n * wide, wide), wide)
+        out[:, place] = own[n, z, core].astype(BF16)
+
+    loop(chunks, store)
+    place = pl.ds(pl.multiple_of(core * half, half), half)
+    last = pltpu.make_async_remote_copy(
+        src_ref=final, dst_ref=out.at[:, place],
+        send_sem=out_sem.at[0], recv_sem=out_sem.at[1],
+        device_id=mate, device_id_type=MESH,
+    )
+    last.start()
+
+    for zp in range(4):
+        r = zp * 2 + x
+        pl.when(has_right & (zp <= z))(lambda r=r: copy_x(0, r, right, core).wait_send())
+        pl.when(has_left & (zp >= z))(lambda r=r: copy_x(1, r, left, core).wait_send())
+        copy_x(2, r, across, core).wait_send()
+        for xp in range(2):
+
+            @pl.when(zp // 2 == 1 - core)
+            def _(r=zp * 2 + xp):
+                copy_x(3, r, mate, core).wait_send()
+
+    def left_behind(n):
+        copy_pre(n).wait_send()
+        copy_hid(n, core).wait_send()
+        copy_rs(n).wait_send()
+        for zp in range(4):
+            pl.when(zp > z)(lambda zp=zp: copy_right(n, zp).wait_send())
+            pl.when(zp < z)(lambda zp=zp: copy_left(n, zp).wait_send())
+
+    loop(chunks, left_behind)
+    last.wait()
+
+
+def fused(tokens, w_up, w_down, mask_up, mask_down):
+    core = lax.axis_index("col")
+    block = w_up.shape[0] * 2 // mask_up.shape[0]
+    rows_up, cols_down = mask_up.shape[0] // 2, mask_down.shape[1] // 2
+    mask_up = lax.dynamic_slice_in_dim(mask_up, core * rows_up, rows_up, 0)
+    mask_down = lax.dynamic_slice_in_dim(mask_down, core * cols_down, cols_down, 1)
+    mask_up = jnp.repeat(mask_up.astype(F32), block, axis=1)
+    mask_down = jnp.repeat(mask_down.astype(F32), block, axis=1)
+    count, feats = tokens.shape
+    wide, depth = WIDE, w_up.shape[0]
+    chunks = w_up.shape[1] // wide
+    few = count // 8
+    dma = pltpu.SemaphoreType.DMA
+    vmem = pl.BlockSpec(memory_space=pltpu.VMEM)
+    hbm = pl.BlockSpec(memory_space=pl.ANY)
+    travel = (chunks, 4, 2, few, wide)
+    return pl.pallas_call(
+        functools.partial(kernel, block),
+        out_shape=jax.ShapeDtypeStruct((few, w_down.shape[1] * 2), BF16),
+        in_specs=[hbm, hbm, hbm, vmem, vmem],
+        out_specs=vmem,
+        scratch_shapes=[
+            pltpu.VMEM((chunks, depth, wide), BF16),
+            pltpu.VMEM((8, 2, count, feats), BF16),
+            pltpu.VMEM((chunks, 2, count, wide), F32),
+            pltpu.VMEM((chunks, count, wide), F32),
+            pltpu.VMEM((chunks, 2, count, wide), BF16),
+            pltpu.VMEM((2, 4, 2, few, wide), F32),
+            pltpu.VMEM(travel, F32),
+            pltpu.VMEM(travel, BF16),
+            pltpu.VMEM(travel, BF16),
+            pltpu.VMEM(travel, BF16),
+            pltpu.VMEM(travel, BF16),
+            pltpu.VMEM(travel, BF16),
+            pltpu.VMEM((few, w_down.shape[1]), BF16),
+            dma,
+            dma((chunks,)),
+            dma((4, 8)),
+            dma((8, 2)),
+            dma((chunks,)), dma((chunks,)),
+            dma((chunks,)), dma((chunks,)),
+            dma((chunks,)), dma((chunks,)),
+            dma((chunks, 4)), dma((chunks, 4)),
+            dma((chunks, 4)), dma((chunks, 4)),
+            dma((2,)),
+        ],
+        compiler_params=pltpu.CompilerParams(
+            collective_id=0, has_side_effects=True, vmem_limit_bytes=63 * 2**20
+        ),
+    )(tokens, w_up, w_down, mask_up, mask_down)
+
+
+WIDE = 512
+
+
+def per_device(tokens, w_up, w_down, mask_up, mask_down):
+    sizes = (lax.axis_size("row"), lax.axis_size("col"))
+    square = w_up.shape[0] == w_up.shape[1] == w_down.shape[0] == w_down.shape[1]
+    if sizes == (8, 2) and square and tokens.shape[0] % 128 == 0 and w_up.shape[1] % WIDE == 0:
+        return fused(tokens, w_up, w_down, mask_up, mask_down)
+    return general(tokens, w_up, w_down, mask_up, mask_down)
 
 
 def solution(mesh):

time: 249 us -> 99.7 us (0.40)
  waiting for transfers between devices: 123 us -> 0 us
  Pallas kernels: 0 us -> 94 us
  matrix products: 70.2 us -> 0 us
  local copies, waits for them, and re-layouts: 28.4 us -> 3.73 us
  between operations: 13.4 us -> 0.03 us
  blocking collectives: 12 us -> 0 us
    pallas_call x0 -> x1, Pallas kernels: none -> 94 us  [fused(): pl.pallas_call(functools.partial(kernel, block), out_shape=jax.ShapeDtype...]
    dot_general x2 -> x0, matrix products: 70.2 us -> none  [the longest x1 36.5 us: per_device(): jnp.dot(hidden, w_down * expand_mask(mask_d, block, w_down.dtype), prefer...]
    reduce_scatter x1 -> x0, waiting for transfers between devices: 66.9 us -> none  [per_device(): lax.psum_scatter(part, 'row', scatter_dimension=0, tiled=True)]
    all_gather x1 -> x0, waiting for transfers between devices: 52.2 us -> none  [per_device(): mine = lax.all_gather(tokens, 'row', axis=1, tiled=True)]
    broadcast_in_dim x2, local copies, waits for them, and re-layouts: 22.3 us -> 0.38 us  [the longest x1 0.19 us: fused(): mask_up = jnp.repeat(mask_up.astype(F32), block, axis=1)]
    all_to_all x2 -> x0, blocking collectives: 12 us -> none  [the longest x1 6.61 us: per_device(): x = lax.all_to_all(mine, 'col', split_axis=1, concat_axis=0, tiled=True)]
    all_to_all x2 -> x0, local copies, waits for them, and re-layouts: 4.22 us -> none  [the longest x1 2.74 us: per_device(): x = lax.all_to_all(mine, 'col', split_axis=1, concat_axis=0, tiled=True)]
    ppermute x1 -> x0, waiting for transfers between devices: 4.15 us -> none  [per_device(): lax.ppermute(pre.astype(jnp.bfloat16), 'col', swap).astype(jnp.float32)]
  transfers between devices with their start and end apart: 3 -> 0, of which waited for: 3 -> 0; matrix products, arithmetic and copies ran while one was open for 0% -> 0% of each run, Pallas kernels for 0% -> 0%
where the time goes in v2:
time: 99.7 us; the launch traced here: 99.4 us
  Pallas kernels  94 us (94%)
  local copies, waits for them, and re-layouts  3.73 us (4%)
  other arithmetic  1.59 us (2%)
    pallas_call x1, Pallas kernels, fused(): pl.pallas_call(functools.partial(kernel, block), out_shape=jax.ShapeDtype...  94 us

profile of v2, /device:TPU:0, one launch (start us, length us, event | category | flops | bytes accessed | tf_op | source)
XLA Modules:
  0.0 99.4 jit_solution(4642107788994913341)
XLA Ops:
  0.0 0.8 dynamic-slice_convert_fusion.1
  0.8 0.1 copy.6
  0.9 0.8 dynamic-slice_convert_fusion
  1.7 0.2 broadcast_in_dim.7
  1.9 0.2 broadcast_in_dim.6
  2.1 1.6 %copy_bitcast_fusion = (f32[32,4096]{1,0:T(8,128)}, f32[32,4096]{1,0:T(8,128)}) fusion(f32[4,8,32,128]{3,2,1,0:T(8,128)S(1)} %bitcast.6, f32[4,8,32,128]{3,2,1,0:T(8,128)S(1)} %bitcast.7), kind=kLoop, calls=%fused_computation | loop fusion | bytes 2097152 | tf_op jit(solution)/shard_map/reshape | solution.py:330
  3.7 94.0 %shard_map.55 = bf16[16,8192]{1,0:T(8,128)(2,1)} custom-call(bf16[128,1024]{1,0:T(8,128)(2,1)} %tokens.1, bf16[4096,4096]{1,0:T(8,128)(2,1)} %w_up.1, bf16[4096,4096]{1,0:T(8,128)(2,1)} %w_down.1, f32[32,4096]{1,0:T(8,128)} %get-tuple-element.6.mask_up, f32[32,4096]{1,0:T(8,128)} %get-tuple-element.5.mask_down), custom_call_target="tpu_custom_call" | custom-call | tf_op jit(solution)/shard_map/pallas_call | solution.py:339
  97.7 1.7 %copy.12 = bf16[16,8192]{1,0:T(8,128)(2,1)} copy(bf16[16,8192]{1,0:T(8,128)(2,1)} %shard_map.55) | data formatting | bytes 524288

commit v3 on v2

--- a/solution.py
+++ b/solution.py
@@ -60,10 +60,11 @@
 ):
     row, core = lax.axis_index("row"), lax.axis_index("col")
     z, x = row // 2, row % 2
-    chunks, depth, wide = w.shape
-    feats = x_all.shape[-1]
+    chunks, _, tall, wide = acc.shape
+    slots, feats, _ = w.shape
     half = chunks * wide
-    count = 8
+    ratio = wide // block
+    tall = tall // 2
 
     def loop(steps, body):
         lax.fori_loop(0, steps, lambda i, _: (body(i), 0)[1], 0)
@@ -71,10 +72,18 @@
     def cols(n):
         return pl.ds(pl.multiple_of(n * wide, wide), wide)
 
-    def load_w(source, n):
-        return pltpu.make_async_copy(source.at[:, cols(n)], w.at[n], w_sem.at[n])
-
-    loop(chunks, lambda n: load_w(w_up, n).start())
+    def load_w(source, part_of, s, n):
+        rows = pl.ds(pl.multiple_of(part_of * feats, feats), feats)
+        return pltpu.make_async_copy(
+            source.at[rows, cols(n)], w.at[s, :, cols(n)], w_sem.at[s, n]
+        )
+
+    def load_up(r, s, n):
+        return load_w(w_up, r - slots * core, s, n)
+
+    def load_down(s, n):
+        return load_w(w_down, s, s, n)
+
     load = pltpu.make_async_copy(tokens, x_all.at[row, core], load_sem)
     load.start()
 
@@ -94,54 +103,59 @@
     pl.semaphore_wait(barrier, 2 + ends)
     load.wait()
 
-    def copy_x(kind, r, device, which):
-        return pltpu.make_async_remote_copy(
-            src_ref=x_all.at[r, which], dst_ref=x_all.at[r, which],
-            send_sem=x_send.at[kind, r], recv_sem=x_recv.at[r, which],
+    def copy_x(kind, r, device, which, h):
+        rows = pl.ds(h * tall, tall)
+        return pltpu.make_async_remote_copy(
+            src_ref=x_all.at[r, which, rows], dst_ref=x_all.at[r, which, rows],
+            send_sem=x_send.at[kind, r, h], recv_sem=x_recv.at[r, which, h],
             device_id=device, device_id_type=MESH,
         )
 
-    def to_mate(zp, xp):
+    def to_mate(zp, xp, h):
         @pl.when(zp // 2 == 1 - core)
         def _():
-            copy_x(3, zp * 2 + xp, mate, core).start()
-
-    def pass_on(zp, go_right, go_left):
+            copy_x(3, zp * 2 + xp, mate, core, h).start()
+
+    def pass_on(zp, go_right, go_left, h):
         r = zp * 2 + x
-        pl.when(go_right)(lambda: copy_x(0, r, right, core).start())
-        pl.when(go_left)(lambda: copy_x(1, r, left, core).start())
-        copy_x(2, r, across, core).start()
-        to_mate(zp, x)
-
-    def arrive(zp, xp):
-        copy_x(2, zp * 2 + xp, across, core).wait_recv()
-
-    pass_on(z, has_right, has_left)
+        pl.when(go_right)(lambda: copy_x(0, r, right, core, h).start())
+        pl.when(go_left)(lambda: copy_x(1, r, left, core, h).start())
+        copy_x(2, r, across, core, h).start()
+        to_mate(zp, x, h)
+
+    def arrive(zp, xp, h):
+        copy_x(2, zp * 2 + xp, across, core, h).wait_recv()
+
+    for h in (0, 1):
+        pass_on(z, has_right, has_left, h)
 
     def step(d):
-        if d < 4:
-
-            @pl.when(z - d >= 0)
+        for h in (0, 1):
+            if d < 4:
+
+                @pl.when(z - d >= 0)
+                def _():
+                    arrive(z - d, x, h)
+                    pass_on(z - d, has_right, False, h)
+
+                @pl.when(z + d <= 3)
+                def _():
+                    arrive(z + d, x, h)
+                    pass_on(z + d, False, has_left, h)
+
+        for h in (0, 1):
+
+            @pl.when(z - (d - 1) >= 0)
             def _():
-                arrive(z - d, x)
-                pass_on(z - d, has_right, False)
-
-            @pl.when(z + d <= 3)
-            def _():
-                arrive(z + d, x)
-                pass_on(z + d, False, has_left)
-
-        @pl.when(z - (d - 1) >= 0)
-        def _():
-            arrive(z - (d - 1), 1 - x)
-            to_mate(z - (d - 1), 1 - x)
-
-        if d > 1:
-
-            @pl.when(z + (d - 1) <= 3)
-            def _():
-                arrive(z + (d - 1), 1 - x)
-                to_mate(z + (d - 1), 1 - x)
+                arrive(z - (d - 1), 1 - x, h)
+                to_mate(z - (d - 1), 1 - x, h)
+
+            if d > 1:
+
+                @pl.when(z + (d - 1) <= 3)
+                def _():
+                    arrive(z + (d - 1), 1 - x, h)
+                    to_mate(z + (d - 1), 1 - x, h)
 
     def copy_pre(n):
         return pltpu.make_async_remote_copy(
@@ -150,44 +164,57 @@
             device_id=mate, device_id_type=MESH,
         )
 
-    def masked(n, start, mask, blocks):
+    def masked(s, first, n, mask, mask_row, mask_col, blocks):
         parts = []
         for j in range(blocks):
-            keep = mask[pl.ds(start + j, 1), cols(n)].astype(BF16)
-            rows = pl.ds(pl.multiple_of((start + j) * block, block), block)
-            parts.append(w[n, rows, :] * keep)
+            rows = pl.ds(pl.multiple_of(first + j * block, block), block)
+            tiles = []
+            for t in range(ratio):
+                place = pl.ds(pl.multiple_of(n * wide + t * block, block), block)
+                keep = mask[mask_row + j, mask_col + t].astype(F32)
+                tiles.append(w[s, rows, place] * jnp.full((block, block), keep, F32).astype(BF16))
+            parts.append(jnp.concatenate(tiles, axis=1))
         return jnp.concatenate(parts, axis=0)
 
-    def up(r, first, last):
-        copy_x(3, r, mate, 1 - core).wait_recv()
+    def up(r, s):
+        for h in (0, 1):
+            copy_x(3, r, mate, 1 - core, h).wait_recv()
         blocks = feats // block
-        start = (r - 4 * core) * blocks
 
         def body(n):
-            if first:
-                load_w(w_up, n).wait()
+            load_up(r, s, n).wait()
             done = jnp.dot(
-                x_all[r].reshape(-1, feats), masked(n, start, mask_up, blocks),
+                x_all[r].reshape(-1, feats),
+                masked(s, 0, n, mask_up, r * blocks, n * ratio, blocks),
                 preferred_element_type=F32,
             ).reshape(acc.shape[1:])
-            acc[n] = done if first else acc[n] + done
-            if last:
+            acc[n] = done if s == 0 else acc[n] + done
+            if s == slots - 1:
                 copy_pre(n).start()
-                load_w(w_down, n).start()
+            load_down(s, n).start()
 
         loop(chunks, body)
 
     low = 2 * core
     near = jnp.clip(z, low, low + 1)
     far = 2 * low + 1 - near
+    order = (near * 2 + x, far * 2 + x, near * 2 + 1 - x, far * 2 + 1 - x)
+
+    def fetch(s):
+        loop(chunks, lambda n: load_up(order[s], s, n).start())
+
+    fetch(0)
     step(1)
+    fetch(1)
     step(2)
-    up(near * 2 + x, True, False)
+    fetch(2)
+    up(order[0], 0)
     step(3)
-    up(far * 2 + x, False, False)
-    up(near * 2 + 1 - x, False, False)
+    fetch(3)
+    up(order[1], 1)
+    up(order[2], 2)
     step(4)
-    up(far * 2 + 1 - x, False, True)
+    up(order[3], 3)
 
     def copy_hid(n, which):
         return pltpu.make_async_remote_copy(
@@ -226,17 +253,21 @@
         )
 
     def down(n):
-        load_w(w_down, n).wait()
+        for s in range(slots):
+            load_down(s, n).wait()
         part[...] = jnp.zeros_like(part)
-        blocks = wide // block
+        per = feats // wide
 
         def body(k):
+            keep = masked(
+                k // per, (k % per) * wide, n, mask_down, k * ratio, (core * chunks + n) * ratio, ratio
+            )
             part[...] += jnp.dot(
-                hid[k].reshape(-1, wide), masked(n, k * blocks, mask_down, blocks),
+                hid[k].reshape(-1, wide), keep,
                 preferred_element_type=F32,
             ).reshape(part.shape)
 
-        loop(depth // wide, body)
+        loop(slots * per, body)
         for zp in range(4):
             for cp in range(2):
                 to_x[n, zp, cp] = part[cp, zp, 1 - x].astype(BF16)
@@ -297,16 +328,17 @@
     )
     last.start()
 
-    for zp in range(4):
-        r = zp * 2 + x
-        pl.when(has_right & (zp <= z))(lambda r=r: copy_x(0, r, right, core).wait_send())
-        pl.when(has_left & (zp >= z))(lambda r=r: copy_x(1, r, left, core).wait_send())
-        copy_x(2, r, across, core).wait_send()
-        for xp in range(2):
-
-            @pl.when(zp // 2 == 1 - core)
-            def _(r=zp * 2 + xp):
-                copy_x(3, r, mate, core).wait_send()
+    for h in (0, 1):
+        for zp in range(4):
+            r = zp * 2 + x
+            pl.when(has_right & (zp <= z))(lambda: copy_x(0, r, right, core, h).wait_send())
+            pl.when(has_left & (zp >= z))(lambda: copy_x(1, r, left, core, h).wait_send())
+            copy_x(2, r, across, core, h).wait_send()
+            for xp in range(2):
+
+                @pl.when(zp // 2 == 1 - core)
+                def _():
+                    copy_x(3, zp * 2 + xp, mate, core, h).wait_send()
 
     def left_behind(n):
         copy_pre(n).wait_send()
@@ -321,13 +353,7 @@
 
 
 def fused(tokens, w_up, w_down, mask_up, mask_down):
-    core = lax.axis_index("col")
     block = w_up.shape[0] * 2 // mask_up.shape[0]
-    rows_up, cols_down = mask_up.shape[0] // 2, mask_down.shape[1] // 2
-    mask_up = lax.dynamic_slice_in_dim(mask_up, core * rows_up, rows_up, 0)
-    mask_down = lax.dynamic_slice_in_dim(mask_down, core * cols_down, cols_down, 1)
-    mask_up = jnp.repeat(mask_up.astype(F32), block, axis=1)
-    mask_down = jnp.repeat(mask_down.astype(F32), block, axis=1)
     count, feats = tokens.shape
     wide, depth = WIDE, w_up.shape[0]
     chunks = w_up.shape[1] // wide
@@ -335,14 +361,15 @@
     dma = pltpu.SemaphoreType.DMA
     vmem = pl.BlockSpec(memory_space=pltpu.VMEM)
     hbm = pl.BlockSpec(memory_space=pl.ANY)
+    smem = pl.BlockSpec(memory_space=pltpu.SMEM)
     travel = (chunks, 4, 2, few, wide)
     return pl.pallas_call(
         functools.partial(kernel, block),
         out_shape=jax.ShapeDtypeStruct((few, w_down.shape[1] * 2), BF16),
-        in_specs=[hbm, hbm, hbm, vmem, vmem],
+        in_specs=[hbm, hbm, hbm, smem, smem],
         out_specs=vmem,
         scratch_shapes=[
-            pltpu.VMEM((chunks, depth, wide), BF16),
+            pltpu.VMEM((4, depth // 4, w_up.shape[1]), BF16),
             pltpu.VMEM((8, 2, count, feats), BF16),
             pltpu.VMEM((chunks, 2, count, wide), F32),
             pltpu.VMEM((chunks, count, wide), F32),
@@ -356,9 +383,9 @@
             pltpu.VMEM(travel, BF16),
             pltpu.VMEM((few, w_down.shape[1]), BF16),
             dma,
-            dma((chunks,)),
-            dma((4, 8)),
-            dma((8, 2)),
+            dma((4, chunks)),
+            dma((4, 8, 2)),
+            dma((8, 2, 2)),
             dma((chunks,)), dma((chunks,)),
             dma((chunks,)), dma((chunks,)),
             dma((chunks,)), dma((chunks,)),
@@ -377,7 +404,7 @@
 
 def per_device(tokens, w_up, w_down, mask_up, mask_down):
     sizes = (lax.axis_size("row"), lax.axis_size("col"))
-    square = w_up.shape[0] == w_up.shape[1] == w_down.shape[0] == w_down.shape[1]
+    square = tokens.shape[1] * 4 == w_up.shape[0] == w_up.shape[1] == w_down.shape[0] == w_down.shape[1]
     if sizes == (8, 2) and square and tokens.shape[0] % 128 == 0 and w_up.shape[1] % WIDE == 0:
         return fused(tokens, w_up, w_down, mask_up, mask_down)
     return general(tokens, w_up, w_down, mask_up, mask_down)

time: 99.7 us -> 95.3 us (0.956)
  Pallas kernels: 94 us -> 91.9 us
  other arithmetic: 1.59 us -> 0 us
    pallas_call x1, Pallas kernels: 94 us -> 91.9 us  [fused(): pl.pallas_call(functools.partial(kernel, block), out_shape=jax.ShapeDtype...]
    reshape x1 -> x0, local copies, waits for them, and re-layouts: 1.6 us -> none  [fused(): mask_down = jnp.repeat(mask_down.astype(F32), block, axis=1)]
    convert_element_type x2 -> x0, other arithmetic: 1.59 us -> none  [the longest x1 0.8 us: fused(): mask_down = jnp.repeat(mask_down.astype(F32), block, axis=1)]
    unnamed x1 -> x2, local copies, waits for them, and re-layouts: 1.67 us -> 3.08 us
where the time goes in v3:
time: 95.3 us; the launch traced here: 95 us
  Pallas kernels  91.9 us (96%)
  local copies, waits for them, and re-layouts  3.08 us (3%)
    pallas_call x1, Pallas kernels, fused(): pl.pallas_call(functools.partial(kernel, block), out_shape=jax.ShapeDtype...  91.9 us
    unnamed x2, local copies, waits for them, and re-layouts  3.08 us

profile of v3, /device:TPU:0, one launch (start us, length us, event | category | flops | bytes accessed | tf_op | source)
XLA Modules:
  0.0 95.0 jit_solution(11751634872319424366)
XLA Ops:
  0.0 1.4 %copy.6.mask_up = s32[64,32]{1,0:T(8,128)} copy(s32[64,32]{0,1:T(8,128)} %param.8) | data formatting | bytes 16384 | tf_op args[3]
  1.4 91.9 %shard_map.55 = bf16[16,8192]{1,0:T(8,128)(2,1)} custom-call(bf16[128,1024]{1,0:T(8,128)(2,1)} %tokens.1, bf16[4096,4096]{1,0:T(8,128)(2,1)} %w_up.1, bf16[4096,4096]{1,0:T(8,128)(2,1)} %w_down.1, s32[64,32]{1,0:T(8,128)} %copy.6.mask_up, s32[32,64]{1,0:T(8,128)} %mask_down.1), custom_call_target="tpu_custom_call" | custom-call | tf_op jit(solution)/shard_map/pallas_call | solution.py:366
  93.3 1.7 %copy.8 = bf16[16,8192]{1,0:T(8,128)(2,1)} copy(bf16[16,8192]{1,0:T(8,128)(2,1)} %shard_map.55) | data formatting | bytes 524288

commit v4 on v3

--- a/solution.py
+++ b/solution.py
@@ -43,7 +43,7 @@
 
 MESH = pl.DeviceIdType.MESH
 BF16, F32 = jnp.bfloat16, jnp.float32
-LAG = 2
+LAG = 1
 
 
 def gelu(v):

time: 95.3 us -> 97.2 us (1.020)
  Pallas kernels: 91.9 us -> 93.8 us
    pallas_call x1, Pallas kernels: 91.9 us -> 93.8 us  [fused(): pl.pallas_call(functools.partial(kernel, block), out_shape=jax.ShapeDtype...]
where the time goes in v4:
time: 97.2 us; the launch traced here: 96.8 us
  Pallas kernels  93.8 us (97%)
  local copies, waits for them, and re-layouts  3.08 us (3%)
    pallas_call x1, Pallas kernels, fused(): pl.pallas_call(functools.partial(kernel, block), out_shape=jax.ShapeDtype...  93.8 us
    unnamed x2, local copies, waits for them, and re-layouts  3.08 us

profile of v4, /device:TPU:0, one launch (start us, length us, event | category | flops | bytes accessed | tf_op | source)
XLA Modules:
  0.0 96.8 jit_solution(7054435989857800665)
XLA Ops:
  0.0 1.4 %copy.6.mask_up = s32[64,32]{1,0:T(8,128)} copy(s32[64,32]{0,1:T(8,128)} %param.8) | data formatting | bytes 16384 | tf_op args[3]
  1.4 93.8 %shard_map.55 = bf16[16,8192]{1,0:T(8,128)(2,1)} custom-call(bf16[128,1024]{1,0:T(8,128)(2,1)} %tokens.1, bf16[4096,4096]{1,0:T(8,128)(2,1)} %w_up.1, bf16[4096,4096]{1,0:T(8,128)(2,1)} %w_down.1, s32[64,32]{1,0:T(8,128)} %copy.6.mask_up, s32[32,64]{1,0:T(8,128)} %mask_down.1), custom_call_target="tpu_custom_call" | custom-call | tf_op jit(solution)/shard_map/pallas_call | solution.py:366
  95.2 1.7 %copy.8 = bf16[16,8192]{1,0:T(8,128)(2,1)} copy(bf16[16,8192]{1,0:T(8,128)(2,1)} %shard_map.55) | data formatting | bytes 524288
